TPU v7x, 32 devices: a whole 2x2x4 slice. The times are simulated.
32 devices in a mesh: mem: 16 (over z, y, core), lat: 2 (over x).
Axes of the slice: x: 2, y: 2, z: 4, core: 2. Of those that a mesh axis runs over, the one named last changes fastest.
Arguments:
- controls: bfloat16 [64, 64, 256, 256], P('mem', None, 'lat'), may hold values from -6 to 6
- spread: bfloat16 [64, 64, 256, 256], P('mem', None, 'lat'), may hold values from -1.5 to 1.5
- classes: int32 [256, 256], P('lat'), may hold values from 0 to 7
- prec_table: float32 [8, 64], replicated, may hold values from 0.25 to 4
- vert_loc: bfloat16 [64, 64], replicated, may hold values from 0 to 1
- lon_loc: bfloat16 [256, 256], replicated, may hold values from 0 to 1
- lat_loc: bfloat16 [256, 256], replicated, may hold values from 0 to 1
Outputs:
- localized: bfloat16 [64, 64, 256, 256], P('mem', None, 'lat')
All inputs are finite; a program needn't handle non-finite values.
Results may differ from a plain program's by a relative error of at most 0.0064.
Values may be sent and summed in bfloat16 or wider, within the bound.
A program may use at most 128 MiB of HBM per device.

v0:
```python
import jax
import jax.numpy as jnp
from jax import lax
from jax.sharding import PartitionSpec as P


def lookup(table, classes):
    numbers = jnp.arange(table.shape[0], dtype=jnp.int32)
    onehot = (classes[None, :, :] == numbers[:, None, None]).astype(jnp.float32)
    return jnp.einsum("kl,kab->lab", table, onehot, precision=lax.Precision.HIGHEST)


def local(controls, spread, classes, prec_table, vert_loc, lon_loc, lat_loc):
    partial_value = jnp.sum(spread.astype(jnp.float32) * controls.astype(jnp.float32), axis=0)
    shares = lax.psum_scatter(partial_value, "mem", scatter_dimension=0, tiled=True)
    level_count = shares.shape[0]
    table_rows = lax.dynamic_slice_in_dim(
        prec_table, lax.axis_index("mem") * level_count, level_count, 1
    )
    weighted_part = shares * lookup(table_rows, classes)
    weighted = lax.all_gather(weighted_part, "mem", axis=0, tiled=True)
    adjoint = (spread.astype(jnp.float32) * weighted[None]).astype(jnp.bfloat16)
    along_lon = jnp.einsum(
        "mlac,bc->mlab", adjoint, lon_loc, preferred_element_type=jnp.float32
    ).astype(jnp.bfloat16)
    sending = jnp.einsum(
        "lj,mjab->mlab", vert_loc, along_lon, preferred_element_type=jnp.float32
    ).astype(jnp.bfloat16)
    return jnp.einsum(
        "ac,mlcb->mlba",
        lat_loc,
        lax.all_to_all(sending, "lat", split_axis=3, concat_axis=2, tiled=True),
        preferred_element_type=jnp.float32,
    ).astype(jnp.bfloat16)


def solution(mesh):
    return jax.shard_map(
        local,
        mesh=mesh,
        in_specs=(
            P("mem", None, "lat", None),
            P("mem", None, "lat", None),
            P("lat", None),
            P(),
            P(),
            P(),
            P(),
        ),
        out_specs=P("mem", None, "lat", None),
        check_vma=False,
    )
```

profile of v0, /device:TPU:0, one launch (start us, length us, event | category | flops | bytes accessed | tf_op | source)
XLA Modules:
  0.0 539.2 jit_solution(17640405347638670509)
XLA Ops:
  6.5 0.0 copy-start
  6.5 0.0 copy-start.5
  6.5 0.0 copy-start.3
  6.5 0.0 reduce-scatter.2.cloned.1.call-start
  6.5 17.7 %fusion = f32[64,128,256]{2,1,0:T(8,128)} fusion(bf16[4,64,128,256]{3,2,1,0:T(8,128)(2,1)} %param.8, bf16[4,64,128,256]{3,2,1,0:T(8,128)(2,1)} %param.7), kind=kLoop, calls=%fused_computation.2 | loop fusion | flops 31457280 | bytes 41943040 | tf_op jit(solution)/shard_map/reduce_sum | solution.py:14
  24.3 0.0 reduce-scatter.2.cloned.1.call-update
  24.3 0.0 all-gather.2.cloned.1.call-start
  24.3 0.0 copy-done.5
  24.3 0.0 copy-done.3
  24.4 0.7 fusion.14
  25.1 105.5 %reduce-scatter.2.cloned.1.call-done = f32[4,128,256]{2,1,0:T(8,128)} async-done(((f32[64,128,256]{2,1,0:T(8,128)}), f32[4,128,256]{2,1,0:T(8,128)}) %reduce-scatter.2.cloned.1.call-update) | async-done | bytes 524304 | tf_op jit(solution)/shard_map/reduce_scatter | solution.py:15
  130.6 2.0 copy_multiply_fusion
  132.6 0.0 all-gather.2.cloned.1.call-update
  132.6 0.0 copy-start.4
  132.6 74.1 %all-gather.2.cloned.1.call-done = f32[64,128,256]{2,1,0:T(8,128)} async-done(((f32[4,128,256]{2,1,0:T(8,128)}), f32[64,128,256]{2,1,0:T(8,128)}) %all-gather.2.cloned.1.call-update) | async-done | bytes 8388624 | tf_op jit(solution)/shard_map/all_gather | solution.py:21
  206.7 16.6 %fusion.1 = bf16[4,64,128,256]{3,2,1,0:T(8,128)(2,1)} fusion(bf16[4,64,128,256]{3,2,1,0:T(8,128)(2,1)} %param.8, f32[64,128,256]{2,1,0:T(8,128)} %all-gather.2.cloned.1.call-done), kind=kLoop, calls=%fused_computation.3 | loop fusion | flops 25165824 | bytes 41943040 | tf_op jit(solution)/shard_map/convert_element_type | solution.py:22
  223.4 0.0 copy-done
  223.4 0.0 copy-done.4
  223.4 19.1 %convert_bitcast_fusion = bf16[4,64,128,256]{3,1,2,0:T(8,128)(2,1)} fusion(bf16[4,64,128,256]{3,2,1,0:T(8,128)(2,1)} %fusion.1, bf16[256,256]{1,0:T(8,128)(2,1)S(1)} %copy-done, bf16[64,64]{1,0:T(8,128)(2,1)S(1)} %copy-done.4), kind=kOutput, calls=%fused_computation.7 | convolution fusion | flops 5385486336 | bytes 33693696 | tf_op jit(solution)/shard_map/lj,mjab->mlab/dot_general | solution.py:26
  242.5 25.8 %copy.25 = bf16[4,64,128,256]{2,1,0,3:T(8,128)(2,1)} copy(bf16[4,64,128,256]{3,1,2,0:T(8,128)(2,1)} %convert_bitcast_fusion) | data formatting | bytes 33554432 | tf_op jit(solution)/shard_map/convert_element_type | solution.py:28
  268.3 188.7 %all_to_all.18 = bf16[4,64,128,256]{2,1,0,3:T(8,128)(2,1)S(1)} all-to-all(bf16[4,64,128,256]{2,1,0,3:T(8,128)(2,1)} %copy.25), channel_id=1, replica_groups=mesh['mem'=16,'lat'=2] {'lat'}, dimensions={3} | all-to-all | bytes 33554432 | tf_op jit(solution)/shard_map/all_to_all | solution.py:32
  457.0 36.5 %copy.41 = bf16[4,64,128,2,128]{2,3,4,1,0:T(2,128)(2,1)} copy(bf16[4,64,128,2,128]{2,1,0,4,3:T(8,128)(2,1)S(1)} %bitcast.29) | data formatting | bytes 33554432 | tf_op jit(solution)/shard_map/all_to_all | solution.py:32
  493.5 0.0 copy-start.2
  493.5 0.0 copy-start.1
  493.5 27.0 %all_to_all.16 = bf16[4,64,256,128]{2,3,1,0:T(8,128)(2,1)} reshape(bf16[4,64,2,128,128]{3,2,4,1,0:T(2,128)(2,1)} %bitcast.30) | data formatting | bytes 33554432 | tf_op jit(solution)/shard_map/all_to_all | solution.py:32
  520.4 0.0 copy-done.2
  520.4 11.9 %convolution_convert_fusion = bf16[4,64,128,256]{3,2,1,0:T(8,128)(2,1)} fusion(bf16[4,64,256,128]{2,3,1,0:T(8,128)(2,1)} %all_to_all.16, bf16[256,256]{1,0:T(8,128)(2,1)S(1)} %copy-done.2), kind=kOutput, calls=%fused_computation.10 | convolution fusion | flops 4303355904 | bytes 33685504 | tf_op jit(solution)/shard_map/ac,mlcb->mlba/dot_general | solution.py:29
  532.4 0.0 copy-done.1
Async XLA Ops:
  6.5 216.8 %copy-start = (bf16[256,256]{1,0:T(8,128)(2,1)S(1)}, bf16[256,256]{1,0:T(8,128)(2,1)}, u32[]{:S(2)}) copy-start(bf16[256,256]{1,0:T(8,128)(2,1)} %param.12) | copy-start | bytes 393220
  6.5 17.8 %copy-start.5 = (f32[8,64]{1,0:T(8,128)S(1)}, f32[8,64]{1,0:T(8,128)}, u32[]{:S(2)}) copy-start(f32[8,64]{1,0:T(8,128)} %param.10) | copy-start | bytes 6148
  6.5 17.8 %copy-start.3 = (s32[128,256]{1,0:T(8,128)S(1)}, s32[128,256]{1,0:T(8,128)}, u32[]{:S(2)}) copy-start(s32[128,256]{1,0:T(8,128)} %param.9) | copy-start | bytes 393220
  6.5 124.1 %reduce-scatter.2.cloned.1.call-start = ((), (), s32[]{:S(2)}) async-start(), calls=%async_computation.2 | async-start | bytes 8912896 | tf_op jit(solution)/shard_map/reduce_scatter | solution.py:15
  24.3 182.5 %all-gather.2.cloned.1.call-start = ((), (), s32[]{:S(2)}) async-start(), calls=%async_computation.3 | async-start | bytes 8912896 | tf_op jit(solution)/shard_map/all_gather | solution.py:21
  132.6 90.8 %copy-start.4 = (bf16[64,64]{1,0:T(8,128)(2,1)S(1)}, bf16[64,64]{1,0:T(8,128)(2,1)}, u32[]{:S(2)}) copy-start(bf16[64,64]{1,0:T(8,128)(2,1)} %param.11) | copy-start | bytes 24580
  493.5 27.0 %copy-start.2 = (bf16[256,256]{1,0:T(8,128)(2,1)S(1)}, bf16[256,256]{1,0:T(8,128)(2,1)}, u32[]{:S(2)}) copy-start(bf16[256,256]{1,0:T(8,128)(2,1)} %param.13) | copy-start | bytes 393220
  493.5 38.9 %copy-start.1 = (bf16[256,256]{1,0:T(8,128)(2,1)S(1)}, bf16[256,256]{1,0:T(8,128)(2,1)}, u32[]{:S(2)}) copy-start(bf16[256,256]{1,0:T(8,128)(2,1)} %param.12) | copy-start | bytes 393220
Sparse Core Ops, SparseCore 0:
  24.4 106.1 reduce-scatter.1
  132.8 73.9 all-gather.1
where the time goes:
time: 541 us; the launch traced here: 539 us
  blocking collectives  189 us (35%)
  waiting for transfers between devices  180 us (33%)
  local copies, waits for them, and re-layouts  89.2 us (16%)
  other arithmetic  36.3 us (7%)
  matrix products  31.8 us (6%)
  between operations  13.4 us (2%)
    all_to_all x1, blocking collectives, local(): lax.all_to_all(sending, 'lat', split_axis=3, concat_axis=2, tiled=True)  189 us
    reduce_scatter x1, waiting for transfers between devices, local(): lax.psum_scatter(partial_value, 'mem', scatter_dimension=0, tiled=True)  106 us
    all_gather x1, waiting for transfers between devices, local(): weighted = lax.all_gather(weighted_part, 'mem', axis=0, tiled=True)  74.1 us
    all_to_all x2, local copies, waits for them, and re-layouts, local(): lax.all_to_all(sending, 'lat', split_axis=3, concat_axis=2, tiled=True)  63.4 us
    convert_element_type x1, local copies, waits for them, and re-layouts, local(): sending = jnp.einsum('lj,mjab->mlab', vert_loc, along_lon, preferred_elem...  25.8 us
    dot_general x1, matrix products, local(): jnp.einsum('lj,mjab->mlab', vert_loc, along_lon, preferred_element_type=j...  19.1 us
    reduce_sum x1, other arithmetic, local(): jnp.sum(spread.astype(jnp.float32) * controls.astype(jnp.float32), axis=0)  17.7 us
    convert_element_type x1, other arithmetic, local(): adjoint = (spread.astype(jnp.float32) * weighted[None]).astype(jnp.bfloat16)  16.6 us
  transfers between devices with their start and end apart: 2, of which 2 were waited for; matrix products, arithmetic and copies ran while one was open for 0% of the time, Pallas kernels for 0%

commit v1 on v0

--- a/solution.py
+++ b/solution.py
@@ -2,6 +2,13 @@
 import jax.numpy as jnp
 from jax import lax
 from jax.sharding import PartitionSpec as P
+
+ticks_pack = lambda row_data, axis_no, d_out: jnp.concatenate(
+    lax.all_to_all(
+        jnp.stack(jnp.split(row_data, lax.axis_size("lat"), axis=axis_no), axis=0), "lat", 0, 0
+    ),
+    d_out,
+)
 
 
 def lookup(table, classes):
@@ -27,10 +34,7 @@
         "lj,mjab->mlab", vert_loc, along_lon, preferred_element_type=jnp.float32
     ).astype(jnp.bfloat16)
     return jnp.einsum(
-        "ac,mlcb->mlba",
-        lat_loc,
-        lax.all_to_all(sending, "lat", split_axis=3, concat_axis=2, tiled=True),
-        preferred_element_type=jnp.float32,
+        "ac,mlcb->mlba", lat_loc, ticks_pack(sending, 3, 2), preferred_element_type=jnp.float32
     ).astype(jnp.bfloat16)
 
 

time: 541 us -> 502 us (0.928)
  local copies, waits for them, and re-layouts: 89.2 us -> 47.5 us
  other arithmetic: 36.3 us -> 42.5 us
    all_to_all x2 -> x0, local copies, waits for them, and re-layouts: 63.4 us -> none  [local(): lax.all_to_all(sending, 'lat', split_axis=3, concat_axis=2, tiled=True)]
    reshape x0 -> x1, local copies, waits for them, and re-layouts: none -> 36.9 us  [jnp.concatenate(lax.all_to_all(jnp.stack(jnp.split(row_data, lax.axis_siz...]
    convert_element_type x1 -> x0, local copies, waits for them, and re-layouts: 25.8 us -> none  [local(): sending = jnp.einsum('lj,mjab->mlab', vert_loc, along_lon, preferred_elem...]
    another operation x0 -> x1, local copies, waits for them, and re-layouts: none -> 10.7 us  [jnp.stack(jnp.split(row_data, lax.axis_size('lat'), axis=axis_no), axis=0)]
    another operation x0 -> x1, other arithmetic: none -> 6.25 us  [jnp.stack(jnp.split(row_data, lax.axis_size('lat'), axis=axis_no), axis=0)]
where the time goes in v1:
time: 502 us
  blocking collectives  187 us (37%)
  waiting for transfers between devices  180 us (36%)
  local copies, waits for them, and re-layouts  47.5 us (9%)
  other arithmetic  42.5 us (8%)
  matrix products  31.8 us (6%)
  between operations  13.5 us (3%)
    all_to_all x1, blocking collectives, lax.all_to_all(jnp.stack(jnp.split(row_data, lax.axis_size('lat'), axis=a...  187 us
    reduce_scatter x1, waiting for transfers between devices, local(): lax.psum_scatter(partial_value, 'mem', scatter_dimension=0, tiled=True)  106 us
    all_gather x1, waiting for transfers between devices, local(): weighted = lax.all_gather(weighted_part, 'mem', axis=0, tiled=True)  74.1 us
    reshape x1, local copies, waits for them, and re-layouts, jnp.concatenate(lax.all_to_all(jnp.stack(jnp.split(row_data, lax.axis_siz...  36.9 us
    dot_general x1, matrix products, local(): jnp.einsum('lj,mjab->mlab', vert_loc, along_lon, preferred_element_type=j...  19.1 us
    reduce_sum x1, other arithmetic, local(): jnp.sum(spread.astype(jnp.float32) * controls.astype(jnp.float32), axis=0)  17.7 us
    convert_element_type x1, other arithmetic, local(): adjoint = (spread.astype(jnp.float32) * weighted[None]).astype(jnp.bfloat16)  16.6 us
    dot_general x1, matrix products, local(): jnp.einsum('ac,mlcb->mlba', lat_loc, ticks_pack(sending, 3, 2), preferred...  12 us
  transfers between devices with their start and end apart: 2, of which 2 were waited for; matrix products, arithmetic and copies ran while one was open for 0% of the time, Pallas kernels for 0%

profile of v1, /device:TPU:0, one launch (start us, length us, event | category | flops | bytes accessed | tf_op | source)
XLA Modules:
  0.0 501.8 jit_solution(6047835043654997496)
XLA Ops:
  6.5 0.0 copy-start
  6.5 0.0 copy-start.5
  6.5 0.0 copy-start.3
  6.5 0.0 reduce-scatter.2.cloned.1.call-start
  6.5 17.7 %fusion = f32[64,128,256]{2,1,0:T(8,128)} fusion(bf16[4,64,128,256]{3,2,1,0:T(8,128)(2,1)} %param.8, bf16[4,64,128,256]{3,2,1,0:T(8,128)(2,1)} %param.7), kind=kLoop, calls=%fused_computation.2 | loop fusion | flops 31457280 | bytes 41943040 | tf_op jit(solution)/shard_map/reduce_sum | solution.py:21
  24.3 0.0 reduce-scatter.2.cloned.1.call-update
  24.3 0.0 all-gather.2.cloned.1.call-start
  24.3 0.0 copy-done.5
  24.3 0.0 copy-done.3
  24.4 0.7 fusion.14
  25.1 105.5 %reduce-scatter.2.cloned.1.call-done = f32[4,128,256]{2,1,0:T(8,128)} async-done(((f32[64,128,256]{2,1,0:T(8,128)}), f32[4,128,256]{2,1,0:T(8,128)}) %reduce-scatter.2.cloned.1.call-update) | async-done | bytes 524304 | tf_op jit(solution)/shard_map/reduce_scatter | solution.py:22
  130.6 2.0 copy_multiply_fusion
  132.6 0.0 all-gather.2.cloned.1.call-update
  132.6 0.0 copy-start.4
  132.6 74.1 %all-gather.2.cloned.1.call-done = f32[64,128,256]{2,1,0:T(8,128)} async-done(((f32[4,128,256]{2,1,0:T(8,128)}), f32[64,128,256]{2,1,0:T(8,128)}) %all-gather.2.cloned.1.call-update) | async-done | bytes 8388624 | tf_op jit(solution)/shard_map/all_gather | solution.py:28
  206.7 16.6 %fusion.1 = bf16[4,64,128,256]{3,2,1,0:T(8,128)(2,1)} fusion(bf16[4,64,128,256]{3,2,1,0:T(8,128)(2,1)} %param.8, f32[64,128,256]{2,1,0:T(8,128)} %all-gather.2.cloned.1.call-done), kind=kLoop, calls=%fused_computation.3 | loop fusion | flops 25165824 | bytes 41943040 | tf_op jit(solution)/shard_map/convert_element_type | solution.py:29
  223.4 0.0 copy-done
  223.4 0.0 copy-done.4
  223.4 19.1 %convert_bitcast_fusion = bf16[4,64,128,256]{3,1,2,0:T(8,128)(2,1)} fusion(bf16[4,64,128,256]{3,2,1,0:T(8,128)(2,1)} %fusion.1, bf16[256,256]{1,0:T(8,128)(2,1)S(1)} %copy-done, bf16[64,64]{1,0:T(8,128)(2,1)S(1)} %copy-done.4), kind=kOutput, calls=%fused_computation.7 | convolution fusion | flops 5385486336 | bytes 33693696 | tf_op jit(solution)/shard_map/lj,mjab->mlab/dot_general | solution.py:33
  242.5 10.7 %slice_bitcast_fusion.1 = (bf16[1,4,64,128,128]{4,2,3,1,0:T(8,128)(2,1)S(1)}, bf16[1,4,64,128,128]{4,2,3,1,0:T(8,128)(2,1)}) fusion(bf16[4,64,128,256]{3,1,2,0:T(8,128)(2,1)} %convert_bitcast_fusion), kind=kLoop, calls=%fused_computation.12 | loop fusion | bytes 33554432 | tf_op jit(solution)/shard_map/stack | solution.py:8
  253.2 6.2 %pad_maximum_fusion = bf16[2,4,64,128,128]{4,2,3,1,0:T(8,128)(2,1)S(1)} fusion(bf16[1,4,64,128,128]{4,2,3,1,0:T(8,128)(2,1)} %get-tuple-element.6, bf16[1,4,64,128,128]{4,2,3,1,0:T(8,128)(2,1)S(1)} %get-tuple-element.5), kind=kLoop, calls=%fused_computation.4 | loop fusion | flops 8388608 | bytes 33554432 | tf_op jit(solution)/shard_map/stack | solution.py:8
  259.4 186.7 %all_to_all.5 = bf16[2,4,64,128,128]{4,2,3,1,0:T(8,128)(2,1)S(1)} all-to-all(bf16[2,4,64,128,128]{4,2,3,1,0:T(8,128)(2,1)S(1)} %pad_maximum_fusion), channel_id=1, replica_groups=mesh['mem'=16,'lat'=2] {'lat'}, dimensions={0} | all-to-all | bytes 33554432 | tf_op jit(solution)/shard_map/all_to_all | solution.py:7
  446.1 0.0 copy-start.2
  446.1 36.9 %copy.24 = bf16[4,64,2,128,128]{4,3,2,1,0:T(8,128)(2,1)} copy(bf16[4,64,2,128,128]{4,1,3,0,2:T(8,128)(2,1)S(1)} %bitcast.29) | data formatting | bytes 33554432 | tf_op jit(solution)/shard_map/reshape | solution.py:6
  483.0 0.0 copy-start.1
  483.0 0.0 copy-done.2
  483.0 12.0 %convolution_convert_fusion = bf16[4,64,128,256]{3,2,1,0:T(8,128)(2,1)} fusion(bf16[4,64,256,128]{3,2,1,0:T(8,128)(2,1)} %bitcast.30, bf16[256,256]{1,0:T(8,128)(2,1)S(1)} %copy-done.2), kind=kOutput, calls=%fused_computation.10 | convolution fusion | flops 4303355904 | bytes 33685504 | tf_op jit(solution)/shard_map/ac,mlcb->mlba/dot_general | solution.py:36
  494.9 0.0 copy-done.1
Async XLA Ops:
  6.5 216.8 %copy-start = (bf16[256,256]{1,0:T(8,128)(2,1)S(1)}, bf16[256,256]{1,0:T(8,128)(2,1)}, u32[]{:S(2)}) copy-start(bf16[256,256]{1,0:T(8,128)(2,1)} %param.12) | copy-start | bytes 393220
  6.5 17.8 %copy-start.5 = (f32[8,64]{1,0:T(8,128)S(1)}, f32[8,64]{1,0:T(8,128)}, u32[]{:S(2)}) copy-start(f32[8,64]{1,0:T(8,128)} %param.10) | copy-start | bytes 6148
  6.5 17.8 %copy-start.3 = (s32[128,256]{1,0:T(8,128)S(1)}, s32[128,256]{1,0:T(8,128)}, u32[]{:S(2)}) copy-start(s32[128,256]{1,0:T(8,128)} %param.9) | copy-start | bytes 393220
  6.5 124.1 %reduce-scatter.2.cloned.1.call-start = ((), (), s32[]{:S(2)}) async-start(), calls=%async_computation.2 | async-start | bytes 8912896 | tf_op jit(solution)/shard_map/reduce_scatter | solution.py:22
  24.3 182.5 %all-gather.2.cloned.1.call-start = ((), (), s32[]{:S(2)}) async-start(), calls=%async_computation.3 | async-start | bytes 8912896 | tf_op jit(solution)/shard_map/all_gather | solution.py:28
  132.6 90.8 %copy-start.4 = (bf16[64,64]{1,0:T(8,128)(2,1)S(1)}, bf16[64,64]{1,0:T(8,128)(2,1)}, u32[]{:S(2)}) copy-start(bf16[64,64]{1,0:T(8,128)(2,1)} %param.11) | copy-start | bytes 24580
  446.1 36.9 %copy-start.2 = (bf16[256,256]{1,0:T(8,128)(2,1)S(1)}, bf16[256,256]{1,0:T(8,128)(2,1)}, u32[]{:S(2)}) copy-start(bf16[256,256]{1,0:T(8,128)(2,1)} %param.13) | copy-start | bytes 393220
  483.0 12.0 %copy-start.1 = (bf16[256,256]{1,0:T(8,128)(2,1)S(1)}, bf16[256,256]{1,0:T(8,128)(2,1)}, u32[]{:S(2)}) copy-start(bf16[256,256]{1,0:T(8,128)(2,1)} %param.12) | copy-start | bytes 393220
Sparse Core Ops, SparseCore 0:
  24.4 106.1 reduce-scatter.1
  132.8 73.9 all-gather.1
